TPU v7x, 32 devices: a whole 2x2x4 slice. The times are simulated.
32 devices in a mesh: groups: 2 (over x), blk: 16 (over z, y, core).
Axes of the slice: x: 2, y: 2, z: 4, core: 2. Of those that a mesh axis runs over, the one named last changes fastest.
Arguments:
- hidden: bfloat16 [16384, 2048], P(('groups', 'blk')), parts along dimension 0, may hold values from -6 to 6
- kept_idx: int32 [32, 128], P(('groups', 'blk')), parts along dimension 0, may hold values from 0 to 511, as said below
- kept_count: int32 [32], P(('groups', 'blk')), parts along dimension 0, may hold values from 0 to 128, as said below
- router: bfloat16 [2048], replicated, may hold values from -0.125 to 0.125
- norm_gain: float32 [2048], replicated, may hold values from 0.25 to 1.75
- qk_gain: float32 [2, 64], replicated, may hold values from 1 to 7
- query_weight: bfloat16 [2048, 2048], P('blk'), may hold values from -1 to 1
- key_weight: bfloat16 [2048, 128], P('blk'), may hold values from -1 to 1
- value_weight: bfloat16 [2048, 128], P('blk'), may hold values from -0.125 to 0.125
- out_weight: bfloat16 [2048, 2048], P('blk'), may hold values from -0.375 to 0.375
Outputs:
- mixed: bfloat16 [16384, 2048], P(('groups', 'blk')), parts along dimension 0
There are 2 independent parts, one for each index of `groups`. A program takes and returns all parts, laid end to end along the dimension named above; an argument that names none is the same for every part. Nothing has to cross between parts.
Inputs may be any that keep to these rules, and one draw needn't show every extreme that they name: `kept_count`: the counts sum to 1024; in every draw some shard's count is exactly 128. `kept_idx`: in row s the first kept_count[s] entries are distinct local token indices in increasing order; entries past the count are 0.
All inputs are finite; a program needn't handle non-finite values.
Results may differ from a plain program's by a relative error of at most 0.01.
Values may be sent and summed in bfloat16 or wider, within the bound.
A program may use at most 128 MiB of HBM per device.

v0:
```python
import math

import jax
import jax.numpy as jnp
from jax import lax
from jax.sharding import PartitionSpec as P

Q_HEADS = 32
KV_HEADS = 2
HEAD = 64
TOK_DEV = 512
KEEP_DEV = 64
CAP = 128


norm_eps = 1e-06
rope_base = 1000000.0


def rms_scale(values, scales):
    return values * lax.rsqrt(jnp.mean(values * values, axis=-1, keepdims=True) + norm_eps) * scales


def rotate(values, angles):
    half_size = values.shape[-1] // 2
    lower_half = values[..., :half_size]
    upper_half = values[..., half_size:]
    cosine = jnp.cos(angles)
    sine_part = jnp.sin(angles)
    return jnp.concatenate(
        [
            lower_half * cosine - upper_half * sine_part,
            upper_half * cosine + lower_half * sine_part,
        ],
        axis=-1,
    )


def attend(query_heads, query_ranks, key_block, value_block, key_ranks, state):
    prev_top, prev_total, prev_acc = state
    length = key_block.shape[0]
    keys_split = key_block.reshape(length, KV_HEADS, HEAD)
    values_split = value_block.reshape(length, KV_HEADS, HEAD)
    scores = jnp.einsum(
        "agch,bgh->gcab", query_heads, keys_split, preferred_element_type=jnp.float32
    ) * (1.0 / math.sqrt(HEAD))
    allowed = key_ranks[None, :] <= query_ranks[:, None]
    masked = jnp.where(allowed, scores, -1e30)
    new_top = jnp.maximum(prev_top, jnp.max(masked, axis=-1))
    weights = jnp.where(allowed, jnp.exp(masked - new_top[..., None]), 0.0)
    factor = jnp.exp(prev_top - new_top)
    new_total = prev_total * factor + jnp.sum(weights, axis=-1)
    new_acc = prev_acc * factor[..., None] + jnp.einsum(
        "gcab,bgh->gcah",
        weights.astype(jnp.bfloat16),
        values_split,
        preferred_element_type=jnp.float32,
    )
    return (new_top, new_total, new_acc)


def make_fold(query_heads, query_ranks, rank_of, state, pieces):
    key_piece, value_piece = pieces
    length = key_piece.shape[0]

    def inner(block_turn, inner_state):
        block_start = block_turn * 512
        key_block = lax.dynamic_slice_in_dim(key_piece, block_start, 512, 0)
        value_block = lax.dynamic_slice_in_dim(value_piece, block_start, 512, 0)
        key_ranks = rank_of(block_start + jnp.arange(512, dtype=jnp.int32))
        return attend(query_heads, query_ranks, key_block, value_block, key_ranks, inner_state)

    return lax.fori_loop(0, length // 512, inner, state)


def body(
    hidden,
    kept_idx,
    kept_count,
    router,
    norm_gain,
    qk_gain,
    query_weight,
    key_weight,
    value_weight,
    out_weight,
):
    shard_count = lax.axis_size("blk")
    device = lax.axis_index("blk")
    width = hidden.shape[1]
    all_lists, all_counts = (
        lax.all_gather(kept_idx, "blk", axis=0, tiled=True),
        lax.all_gather(kept_count, "blk", axis=0, tiled=True),
    )
    starts = jnp.cumsum(all_counts) - all_counts
    own_start = starts[device]
    own_count = all_counts[device]
    list_slots = jnp.arange(CAP, dtype=jnp.int32)
    is_valid = list_slots < own_count
    token_rows = hidden[kept_idx[0]]
    gate_value = jax.nn.sigmoid(jnp.dot(token_rows, router, preferred_element_type=jnp.float32))
    slot_count = (CAP + shard_count - 1) // shard_count
    outgoing = jnp.where(is_valid[:, None], token_rows, jnp.zeros_like(token_rows))
    outgoing = jnp.roll(outgoing.reshape(slot_count, shard_count, width), own_start, axis=1)
    incoming = lax.all_to_all(outgoing, "blk", split_axis=1, concat_axis=1, tiled=True)
    query_ranks = device + jnp.arange(KEEP_DEV, dtype=jnp.int32) * shard_count
    source_ends = starts + all_counts
    source = jnp.sum((source_ends[None, :] <= query_ranks[:, None]).astype(jnp.int32), axis=1)
    within = query_ranks - starts[source]
    flat_index = within // shard_count * shard_count + source
    kept_rows = incoming.reshape(slot_count * shard_count, width)[flat_index]
    positions = source * TOK_DEV + all_lists[source, within]
    row_total = kept_rows.shape[0]
    normed = rms_scale(kept_rows.astype(jnp.float32), norm_gain).astype(jnp.bfloat16)
    query_cols = Q_HEADS * HEAD
    kv_cols = KV_HEADS * HEAD
    full_query, full_key, full_value, full_out = (
        lax.all_gather(query_weight, "blk", axis=0, tiled=True),
        lax.all_gather(key_weight, "blk", axis=0, tiled=True),
        lax.all_gather(value_weight, "blk", axis=0, tiled=True),
        lax.all_gather(out_weight, "blk", axis=0, tiled=True),
    )
    query_lin = jnp.dot(normed, full_query, preferred_element_type=jnp.float32)
    key_lin = jnp.dot(normed, full_key, preferred_element_type=jnp.float32)
    value_lin = jnp.dot(normed, full_value, preferred_element_type=jnp.float32)
    half_size = HEAD // 2
    rotation_rates = rope_base ** (-(jnp.arange(half_size, dtype=jnp.float32) * 2.0 / HEAD))
    angles = (positions.astype(jnp.float32)[:, None] * rotation_rates[None, :])[:, None, :]
    query_heads = rotate(
        rms_scale(query_lin.reshape(row_total, Q_HEADS, HEAD), qk_gain[0]), angles
    ).astype(jnp.bfloat16)
    key_heads = rotate(
        rms_scale(key_lin.reshape(row_total, KV_HEADS, HEAD), qk_gain[1]), angles
    ).astype(jnp.bfloat16)
    query_heads = query_heads.reshape(row_total, KV_HEADS, Q_HEADS // KV_HEADS, HEAD)
    key_flat = key_heads.reshape(row_total, kv_cols)
    value_flat = value_lin.astype(jnp.bfloat16)
    group_size = Q_HEADS // KV_HEADS
    start_state = (
        jnp.full((KV_HEADS, group_size, row_total), -1e30, jnp.float32),
        jnp.zeros((KV_HEADS, group_size, row_total), jnp.float32),
        jnp.zeros((KV_HEADS, group_size, row_total, HEAD), jnp.float32),
    )

    def strided_rank(slots_seen):
        return slots_seen // KEEP_DEV + slots_seen % KEEP_DEV * shard_count

    final_top, final_total, final_acc = make_fold(
        query_heads,
        query_ranks,
        strided_rank,
        start_state,
        (
            lax.all_gather(key_flat, "blk", axis=0, tiled=True),
            lax.all_gather(value_flat, "blk", axis=0, tiled=True),
        ),
    )
    attended = (
        (final_acc / final_total[..., None])
        .transpose(2, 0, 1, 3)
        .reshape(row_total, query_cols)
        .astype(jnp.bfloat16)
    )
    update = jnp.dot(attended, full_out, preferred_element_type=jnp.float32)
    update = update.astype(jnp.bfloat16)
    slot_grid = (
        jnp.arange(slot_count, dtype=jnp.int32)[:, None] * shard_count
        + jnp.mod(device - starts, shard_count)[None, :]
    )
    back_valid = slot_grid < all_counts[None, :]
    local_place = (starts[None, :] + slot_grid - device) // shard_count
    clipped = jnp.where(back_valid, local_place, 0)
    back_rows = jnp.where(back_valid[..., None], update[clipped], jnp.zeros((), jnp.bfloat16))
    returned = lax.all_to_all(back_rows, "blk", split_axis=1, concat_axis=1, tiled=True)
    returned = jnp.roll(returned, -own_start, axis=1).reshape(slot_count * shard_count, width)
    final = (
        token_rows.astype(jnp.float32) + gate_value[:, None] * returned.astype(jnp.float32)
    ).astype(jnp.bfloat16)
    target = jnp.where(is_valid, kept_idx[0], TOK_DEV)
    return hidden.at[target].set(final, mode="drop")


def solution(mesh):
    placed = (
        P(("groups", "blk"), None),
        P(("groups", "blk"), None),
        P(("groups", "blk")),
        P(),
        P(),
        P(),
        P("blk", None),
        P("blk", None),
        P("blk", None),
        P("blk", None),
    )
    return jax.shard_map(
        body, mesh=mesh, in_specs=placed, out_specs=P(("groups", "blk"), None), check_vma=False
    )
```

profile of v0, /device:TPU:0, one launch (start us, length us, event | category | flops | bytes accessed | tf_op | source)
XLA Modules:
  0.0 215.0 jit_solution(3244303445806012775)
XLA Ops:
  6.5 1.6 copy.93
  8.2 0.7 all-gather.6.cloned.1.call-update
  9.6 0.6 dynamic-slice
  10.2 0.7 dynamic-update-slice
  10.9 13.8 %all-reduce = s32[16]{0:T(128)S(1)} all-reduce(s32[16]{0:T(128)S(1)} %dynamic-update-slice), channel_id=1, replica_groups=mesh['groups'=2,'blk'=16] {'blk'}, use_global_device_ids=true, to_apply=%add | all-reduce | flops 16 | bytes 128
  25.0 0.6 dynamic_slice.30
  27.6 0.6 dynamic_slice.29
  28.2 0.6 fusion.45
  28.9 0.9 gather_fusion
  29.8 0.6 add_compare_fusion
  30.4 0.3 copy_select_fusion.1
  30.8 1.0 fusion.30
  31.8 3.6 %all-to-all-start = ((bf16[8,16,2048]{2,0,1:T(8,128)(2,1)}), bf16[8,16,2048]{2,0,1:T(8,128)(2,1)S(1)}, u32[]{:S(2)}, u32[]{:S(2)}) async-start(bf16[8,16,2048]{2,0,1:T(8,128)(2,1)} %fusion.30), calls=%async_computation | async-start | bytes 1048576 | tf_op jit(solution)/shard_map/all_to_all | solution.py:105
  35.5 0.8 gather_fusion.1
  36.4 25.9 %all-gather = s32[16,1,128]{2,1,0:T(1,128)S(1)} all-gather(s32[1,1,128]{2,1,0:T(1,128)S(1)} %bitcast.125), channel_id=1, replica_groups=mesh['groups'=2,'blk'=16] {'blk'}, dimensions={0}, use_global_device_ids=true | all-gather | bytes 8704 | tf_op jit(solution)/shard_map/all_gather | solution.py:92
  62.3 0.8 gather_fusion.3
  63.5 23.3 %all_gather.29 = bf16[2048,128]{1,0:T(8,128)(2,1)S(1)} all-gather(bf16[128,128]{1,0:T(8,128)(2,1)S(1)} %copy-done.3), channel_id=1, replica_groups=mesh['groups'=2,'blk'=16] {'blk'}, dimensions={0}, use_global_device_ids=true | all-gather | bytes 557056 | tf_op jit(solution)/shard_map/all_gather | solution.py:120
  86.8 19.3 %all_gather.25 = bf16[2048,128]{1,0:T(8,128)(2,1)S(1)} all-gather(bf16[128,128]{1,0:T(8,128)(2,1)S(1)} %copy-done.4), channel_id=1, replica_groups=mesh['groups'=2,'blk'=16] {'blk'}, dimensions={0}, use_global_device_ids=true | all-gather | bytes 557056 | tf_op jit(solution)/shard_map/all_gather | solution.py:119
  106.1 0.3 copy.56
  106.4 0.7 gather_fusion.2
  107.3 0.3 fusion.53
  108.4 0.3 convolution_convert_fusion.1
  108.7 20.5 %all_gather.30 = bf16[1024,128]{1,0:T(8,128)(2,1)S(1)} all-gather(bf16[64,128]{1,0:T(8,128)(2,1)S(1)} %convolution_convert_fusion.1), channel_id=1, replica_groups=mesh['groups'=2,'blk'=16] {'blk'}, dimensions={0}, use_global_device_ids=true | all-gather | bytes 278528 | tf_op jit(solution)/shard_map/all_gather | solution.py:155
  129.1 20.5 %all_gather.27 = bf16[1024,128]{1,0:T(8,128)(2,1)S(1)} all-gather(bf16[64,128]{1,0:T(8,128)(2,1)S(1)} %convert_element_type.65), channel_id=1, replica_groups=mesh['groups'=2,'blk'=16] {'blk'}, dimensions={0}, use_global_device_ids=true | all-gather | bytes 278528 | tf_op jit(solution)/shard_map/all_gather | solution.py:154
  149.6 5.0 %fusion.51 = f32[64,2048]{1,0:T(8,128)S(1)} fusion(bf16[2048,2048]{1,0:T(8,128)(2,1)} %all-gather.4.cloned.1.call-done, bf16[64,2048]{1,0:T(8,128)(2,1)S(1)} %gather_fusion.2, f32[2048]{0:T(1024)S(1)} %copy-done.2, f32[64]{0:T(128)S(1)} %add_rsqrt_fusion.2), kind=kOutput, calls=%fused_computation.132 | convolution fusion | flops 537395200 | bytes 9183488 | tf_op jit(solution)/shard_map/dot_general | solution.py:123
  154.6 0.4 reshape.541
  155.0 0.3 multiply_reduce_fusion
  155.4 0.3 multiply_multiply_fusion
  155.8 0.5 subtract_convert_fusion
  156.7 0.3 pad_maximum_fusion
  157.1 19.5 %while.20 = (s32[]{:T(128)}, f32[2,16,64]{2,1,0:T(8,128)S(1)}, f32[2,16,64]{2,1,0:T(8,128)S(1)}, f32[2,16,64,64]{3,2,1,0:T(8,128)S(1)}, bf16[1024,128]{1,0:T(8,1...) while((s32[]{:T(128)}, f32[2,16,64]{2,1,0:T(8,128)S(1)}, ...), condition=%wide.region_8.10_spmd.clone, body=%wide.region_5.9_spmd.clone.sunk | while | flops 282514560 | bytes 15471291 | solution.py:73
  157.3 2.7 %fusion.79 = (f32[2,16,64]{2,1,0:T(8,128)S(1)}, f32[2,512,64,16]{1,2,3,0:T(8,128)}) fusion(pred[64,512]{1,0:T(8,128)(4,1)S(1)} %broadcast_compare_fusion.2, bf16[512,2,64,1]{0,2,3,1:T(8,128)(2,1)S(1)} %bitcast.117, bf16[64,2,16,64]{3,0,2,1:T(8,128)(2,1)S(1)} %get-tuple-element.414), kind=kOutput, calls=%fused_computation.9.clone.1 | convolution fusion | flops 137361408 | bytes 4628480 | tf_op jit(solution)/shard_map/while/body/eval_jaxpr/agch,bgh->gcab/dot_general | solution.py:44
  160.0 3.4 %fusion.80 = f32[2,16,64]{2,1,0:T(8,128)S(1)} fusion(f32[2,512,64,16]{1,2,3,0:T(8,128)} %get-tuple-element.381, f32[2,16,64]{2,1,0:T(8,128)S(1)} %select_maximum_fusion.2, pred[64,512]{1,0:T(8,128)(4,1)S(1)} %broadcast_compare_fusion.2), kind=kLoop, calls=%fused_computation.11.clone.1 | loop fusion | flops 5240832 | bytes 4243456 | tf_op jit(solution)/shard_map/while/body/eval_jaxpr/reduce_sum | solution.py:52
  163.6 3.1 %fusion.82 = f32[2,16,64,64]{3,2,1,0:T(8,128)S(1)} fusion(bf16[512,2,64,1]{0,2,3,1:T(8,128)(2,1)S(1)} %bitcast.120, f32[2,512,64,16]{1,2,3,0:T(8,128)} %get-tuple-element.381, f32[2,16,64]{2,1,0:T(8,128)S(1)} %select_maximum_fusion.2, pred[64,512]{1,0:T(8,128)(4,1)S(1)} %broadcast_compare_fusion.2, f32[2,16,64,64]{3,2,1,0:T(8,128)S(1)} %get-tuple-element.400, ...), kind=kOutput, calls=%fused_computation.14.clone.1 | convolution fusion | flops 139853824 | bytes 5423105 | tf_op jit(solution)/shard_map/while/body/eval_jaxpr/gcab,bgh->gcah/dot_general | solution.py:53
  167.0 2.7 %fusion.79 = (f32[2,16,64]{2,1,0:T(8,128)S(1)}, f32[2,512,64,16]{1,2,3,0:T(8,128)}) fusion(pred[64,512]{1,0:T(8,128)(4,1)S(1)} %broadcast_compare_fusion.2, bf16[512,2,64,1]{0,2,3,1:T(8,128)(2,1)S(1)} %bitcast.117, bf16[64,2,16,64]{3,0,2,1:T(8,128)(2,1)S(1)} %get-tuple-element.414), kind=kOutput, calls=%fused_computation.9.clone.1 | convolution fusion | flops 137361408 | bytes 4628480 | tf_op jit(solution)/shard_map/while/body/eval_jaxpr/agch,bgh->gcab/dot_general | solution.py:44
  169.7 3.5 %fusion.80 = f32[2,16,64]{2,1,0:T(8,128)S(1)} fusion(f32[2,512,64,16]{1,2,3,0:T(8,128)} %get-tuple-element.381, f32[2,16,64]{2,1,0:T(8,128)S(1)} %select_maximum_fusion.2, pred[64,512]{1,0:T(8,128)(4,1)S(1)} %broadcast_compare_fusion.2), kind=kLoop, calls=%fused_computation.11.clone.1 | loop fusion | flops 5240832 | bytes 4243456 | tf_op jit(solution)/shard_map/while/body/eval_jaxpr/reduce_sum | solution.py:52
  173.4 3.1 %fusion.82 = f32[2,16,64,64]{3,2,1,0:T(8,128)S(1)} fusion(bf16[512,2,64,1]{0,2,3,1:T(8,128)(2,1)S(1)} %bitcast.120, f32[2,512,64,16]{1,2,3,0:T(8,128)} %get-tuple-element.381, f32[2,16,64]{2,1,0:T(8,128)S(1)} %select_maximum_fusion.2, pred[64,512]{1,0:T(8,128)(4,1)S(1)} %broadcast_compare_fusion.2, f32[2,16,64,64]{3,2,1,0:T(8,128)S(1)} %get-tuple-element.400, ...), kind=kOutput, calls=%fused_computation.14.clone.1 | convolution fusion | flops 139853824 | bytes 5423105 | tf_op jit(solution)/shard_map/while/body/eval_jaxpr/gcab,bgh->gcah/dot_general | solution.py:53
  176.5 0.3 fusion.31
  176.9 0.3 copy.63
  177.2 0.5 convert_element_type.69
  177.7 5.0 %convolution_convert_fusion = bf16[64,2048]{1,0:T(8,128)(2,1)S(1)} fusion(bf16[64,2048]{1,0:T(8,128)(2,1)S(1)} %convert_element_type.69, bf16[2048,2048]{1,0:T(8,128)(2,1)} %all-gather.6.cloned.1.call-done), kind=kOutput, calls=%fused_computation.38 | convolution fusion | flops 537001984 | bytes 8912896 | tf_op jit(solution)/shard_map/dot_general | solution.py:164
  182.7 0.9 gather_fusion.4
  183.6 1.1 copy_select_fusion
  184.7 3.8 %all-to-all-start.1 = ((bf16[8,16,2048]{2,0,1:T(8,128)(2,1)}), bf16[8,16,2048]{2,0,1:T(8,128)(2,1)S(1)}, u32[]{:S(2)}, u32[]{:S(2)}) async-start(bf16[8,16,2048]{2,0,1:T(8,128)(2,1)} %copy_select_fusion), calls=%async_computation.1 | async-start | bytes 1048576 | tf_op jit(solution)/shard_map/all_to_all | solution.py:174
  189.2 0.2 fusion.22
  189.4 13.1 %all-to-all-done.1 = bf16[8,16,2048]{2,0,1:T(8,128)(2,1)S(1)} async-done(((bf16[8,16,2048]{2,0,1:T(8,128)(2,1)}), bf16[8,16,2048]{2,0,1:T(8,128)(2,1)S(1)}, u32[]{:S(2)}, u32[]{:S(2)}) %all-to-all-start.1) | async-done | bytes 524320 | tf_op jit(solution)/shard_map/all_to_all | solution.py:174
  202.8 0.6 copy.65
  203.6 4.6 %scatter_fusion = bf16[512,2048]{1,0:T(8,128)(2,1)} fusion(bf16[512,2048]{1,0:T(8,128)(2,1)} %copy-done, s32[128]{0:T(128)S(1)} %get-tuple-element.323, bf16[128,2048]{1,0:T(8,128)(2,1)S(1)} %fusion.24), kind=kCustom, calls=%fused_computation.5 | custom fusion | bytes 1573376 | tf_op jit(solution)/shard_map/scatter | solution.py:180
  (81 shorter events, 3.5 us)
Async XLA Ops:
  6.5 3.1 %copy-start.8 = (u32[32]{0:T(128)S(1)}, u32[32]{0:T(128)}, u32[]{:S(2)}) copy-start(u32[32]{0:T(128)} %constant.259) | copy-start | bytes 388
  6.5 21.7 %copy-start.6 = (s32[1,128]{1,0:T(1,128)S(1)}, s32[1,128]{1,0:T(1,128)}, u32[]{:S(2)}) copy-start(s32[1,128]{1,0:T(1,128)} %param.15) | copy-start | bytes 1540
  6.5 143.1 %all-gather.4.cloned.1.call-start = ((), (), s32[]{:S(2)}) async-start(), calls=%async_computation.2 | async-start | bytes 8912896 | tf_op jit(solution)/shard_map/all_gather | solution.py:118
  8.2 23.6 %copy-start = (bf16[512,2048]{1,0:T(8,128)(2,1)}, bf16[512,2048]{1,0:T(8,128)(2,1)S(1)}, u32[]{:S(2)}) copy-start(bf16[512,2048]{1,0:T(8,128)(2,1)S(1)} %copy.93) | copy-start | bytes 6291460
  8.2 169.5 %all-gather.6.cloned.1.call-start = ((), (), s32[]{:S(2)}) async-start(), calls=%async_computation.3 | async-start | bytes 8912896 | tf_op jit(solution)/shard_map/all_gather | solution.py:121
  28.8 34.3 %copy-start.7 = (f32[2,64]{1,0:T(2,128)S(1)}, f32[2,64]{1,0:T(2,128)}, u32[]{:S(2)}) copy-start(f32[2,64]{1,0:T(2,128)} %param.19) | copy-start | bytes 1540
  28.8 34.7 %copy-start.3 = (bf16[128,128]{1,0:T(8,128)(2,1)S(1)}, bf16[128,128]{1,0:T(8,128)(2,1)}, u32[]{:S(2)}) copy-start(bf16[128,128]{1,0:T(8,128)(2,1)} %param.22) | copy-start | bytes 98308
  28.9 57.9 %copy-start.4 = (bf16[128,128]{1,0:T(8,128)(2,1)S(1)}, bf16[128,128]{1,0:T(8,128)(2,1)}, u32[]{:S(2)}) copy-start(bf16[128,128]{1,0:T(8,128)(2,1)} %param.21) | copy-start | bytes 98308
  30.8 76.5 %copy-start.2 = (f32[2048]{0:T(1024)S(1)}, f32[2048]{0:T(1024)}, u32[]{:S(2)}) copy-start(f32[2048]{0:T(1024)} %param.18) | copy-start | bytes 24580
  31.8 74.3 %all-to-all-start = ((bf16[8,16,2048]{2,0,1:T(8,128)(2,1)}), bf16[8,16,2048]{2,0,1:T(8,128)(2,1)S(1)}, u32[]{:S(2)}, u32[]{:S(2)}) async-start(bf16[8,16,2048]{2,0,1:T(8,128)(2,1)} %fusion.30), calls=%async_computation | async-start | bytes 1048576 | tf_op jit(solution)/shard_map/all_to_all | solution.py:105
  155.4 1.6 copy-start.1
  182.7 6.5 %copy-start.5 = (bf16[2048]{0:T(1024)(128)(2,1)S(1)}, bf16[2048]{0:T(1024)(128)(2,1)}, u32[]{:S(2)}) copy-start(bf16[2048]{0:T(1024)(128)(2,1)} %param.17) | copy-start | bytes 12292
  184.7 17.8 %all-to-all-start.1 = ((bf16[8,16,2048]{2,0,1:T(8,128)(2,1)}), bf16[8,16,2048]{2,0,1:T(8,128)(2,1)S(1)}, u32[]{:S(2)}, u32[]{:S(2)}) async-start(bf16[8,16,2048]{2,0,1:T(8,128)(2,1)} %copy_select_fusion), calls=%async_computation.1 | async-start | bytes 1048576 | tf_op jit(solution)/shard_map/all_to_all | solution.py:174
Sparse Core Ops, SparseCore 0:
  9.5 84.1 all-gather.3
  95.8 77.4 all-gather.5
where the time goes:
time: 216 us; the launch traced here: 215 us
  blocking collectives  123 us (57%)
  matrix products  22.3 us (10%)
  between operations  17 us (8%)
  local copies, waits for them, and re-layouts  16.5 us (8%)
  other arithmetic  14.6 us (7%)
  waiting for transfers between devices  13.8 us (6%)
  starting transfers between devices  7.41 us (3%)
    all_gather x1, blocking collectives, body(): lax.all_gather(kept_idx, 'blk', axis=0, tiled=True)  25.9 us
    all_gather x1, blocking collectives, body(): lax.all_gather(value_weight, 'blk', axis=0, tiled=True)  23.3 us
    all_gather x1, blocking collectives, body(): lax.all_gather(value_flat, 'blk', axis=0, tiled=True)  20.5 us
    all_gather x1, blocking collectives, body(): lax.all_gather(key_flat, 'blk', axis=0, tiled=True)  20.5 us
    all_gather x1, blocking collectives, body(): lax.all_gather(key_weight, 'blk', axis=0, tiled=True)  19.3 us
    unnamed x1, blocking collectives  13.8 us
    all_to_all x1, waiting for transfers between devices, body(): lax.all_to_all(back_rows, 'blk', split_axis=1, concat_axis=1, tiled=True)  13.1 us
    reduce_sum x2, other arithmetic, attend(): new_total = prev_total * factor + jnp.sum(weights, axis=-1)  6.96 us
  transfers between devices with their start and end apart: 4, of which 1 were waited for; matrix products, arithmetic and copies ran while one was open for 18% of the time, Pallas kernels for 0%

commit v1 on v0

--- a/solution.py
+++ b/solution.py
@@ -1,8 +1,11 @@
+import functools
 import math
 
 import jax
 import jax.numpy as jnp
 from jax import lax
+from jax.experimental import pallas as pl
+from jax.experimental.pallas import tpu as pltpu
 from jax.sharding import PartitionSpec as P
 
 Q_HEADS = 32
@@ -11,6 +14,8 @@
 TOK_DEV = 512
 KEEP_DEV = 64
 CAP = 128
+MESH = pl.DeviceIdType.MESH
+VM = pl.BlockSpec(memory_space=pltpu.VMEM)
 
 
 norm_eps = 1e-06
@@ -34,6 +39,319 @@
         ],
         axis=-1,
     )
+
+
+def greet(peers):
+    barrier = pltpu.get_barrier_semaphore()
+    for peer in peers:
+        pl.semaphore_signal(barrier, inc=1, device_id={"blk": peer}, device_id_type=MESH)
+    pl.semaphore_wait(barrier, len(peers))
+
+
+def exchange_kernel(n, split, *refs):
+    count = len(split)
+    ins, outs = refs[:count], refs[count : 2 * count]
+    send_sem, recv_sem = refs[2 * count :]
+    me = lax.axis_index("blk")
+
+    def block(i, d):
+        if not split[i]:
+            return ins[i]
+        width = outs[i].shape[-1]
+        return ins[i].at[:, pl.ds(pl.multiple_of(d * width, width), width)]
+
+    greet([lax.rem(me + o, n) for o in range(1, n)])
+    copies = []
+    for o in range(1, n):
+        dest = lax.rem(me + o, n)
+        for i in range(count):
+            copy = pltpu.make_async_remote_copy(
+                src_ref=block(i, dest),
+                dst_ref=outs[i].at[me],
+                send_sem=send_sem.at[i, o],
+                recv_sem=recv_sem.at[i, o],
+                device_id={"blk": dest},
+                device_id_type=MESH,
+            )
+            copy.start()
+            copies.append(copy)
+    for i in range(count):
+        outs[i][me] = block(i, me)[...]
+    for o in range(1, n):
+        source = lax.rem(me + n - o, n)
+        for i in range(count):
+            pltpu.make_async_remote_copy(
+                src_ref=block(i, me),
+                dst_ref=outs[i].at[source],
+                send_sem=send_sem.at[i, o],
+                recv_sem=recv_sem.at[i, o],
+                device_id={"blk": source},
+                device_id_type=MESH,
+            ).wait_recv()
+    for copy in copies:
+        copy.wait_send()
+
+
+def exchange(n, arrays, split, collective_id):
+    outs = []
+    for a, s in zip(arrays, split):
+        shape = (n, a.shape[0], a.shape[1] // n if s else a.shape[1])
+        outs.append(jax.ShapeDtypeStruct(shape, a.dtype))
+    return pl.pallas_call(
+        functools.partial(exchange_kernel, n, split),
+        out_shape=outs,
+        in_specs=[VM] * len(arrays),
+        out_specs=[VM] * len(arrays),
+        scratch_shapes=[
+            pltpu.SemaphoreType.DMA((len(arrays), n)),
+            pltpu.SemaphoreType.DMA((len(arrays), n)),
+        ],
+        compiler_params=pltpu.CompilerParams(collective_id=collective_id, has_side_effects=True),
+    )(*arrays)
+
+
+def scatter_sum_kernel(n, pieces, classes, *refs):
+    kinds = len(classes)
+    ins, outs = refs[:pieces], refs[pieces : pieces + kinds]
+    scratch = refs[pieces + kinds :]
+    chips = n // 2
+    arm = chips // 2
+    me = lax.axis_index("blk")
+    chip, core = me // 2, me % 2
+    side, row = chip % 2, chip // 2
+    place = row * (1 - side) + (chips - 1 - row) * side
+
+    def device(position, on_core):
+        q = lax.rem(position + 2 * chips, chips)
+        far = q // arm
+        chip_id = 2 * (q * (1 - far) + (chips - 1 - q) * far) + far
+        return chip_id * 2 + on_core
+
+    partner = chip * 2 + 1 - core
+    ahead, behind = device(place + 1, core), device(place - 1, core)
+    greet([partner, ahead, behind])
+
+    bufs = [scratch[8 * i : 8 * i + 8] for i in range(kinds)]
+    units = [(i, u) for i, c in enumerate(classes) for u in range(c[1])]
+
+    def target(step, u):
+        return place - 1 - step if u % 2 == 0 else place + 1 + step
+
+    def pair_copy(step, i, u):
+        pair_out, pair_in, _, _, ps, pr, _, _ = bufs[i]
+        return pltpu.make_async_remote_copy(
+            src_ref=pair_out.at[step, u],
+            dst_ref=pair_in.at[step, u],
+            send_sem=ps.at[step, u],
+            recv_sem=pr.at[step, u],
+            device_id={"blk": partner},
+            device_id_type=MESH,
+        )
+
+    def ring_copy(step, i, u):
+        _, _, ring_out, ring_in, _, _, rs, rr = bufs[i]
+        return pltpu.make_async_remote_copy(
+            src_ref=ring_out.at[step, u],
+            dst_ref=ring_in.at[step, u],
+            send_sem=rs.at[step, u],
+            recv_sem=rr.at[step, u],
+            device_id={"blk": ahead if u % 2 == 0 else behind},
+            device_id_type=MESH,
+        )
+
+    def pair_send(step):
+        for i, u in units:
+            chunk = classes[i][0]
+            bufs[i][0][step, u] = chunk(ins, device(target(step, u), 1 - core), u).astype(jnp.bfloat16)
+            pair_copy(step, i, u).start()
+
+    pair_send(0)
+    for step in range(chips):
+        if step + 1 < chips:
+            pair_send(step + 1)
+        for i, u in units:
+            chunk = classes[i][0]
+            total = chunk(ins, device(target(step, u), core), u)
+            pair_copy(step, i, u).wait_recv()
+            total = total + bufs[i][1][step, u].astype(jnp.float32)
+            if step > 0:
+                ring_copy(step - 1, i, u).wait_recv()
+                total = total + bufs[i][3][step - 1, u].astype(jnp.float32)
+            if step + 1 < chips:
+                bufs[i][2][step, u] = total.astype(jnp.bfloat16)
+                ring_copy(step, i, u).start()
+            else:
+                outs[i][u] = total.astype(outs[i].dtype)
+    for step in range(chips):
+        for i, u in units:
+            pair_copy(step, i, u).wait_send()
+            if step + 1 < chips:
+                ring_copy(step, i, u).wait_send()
+
+
+def scatter_sum(n, arrays, classes, out_types, collective_id):
+    chips = n // 2
+    scratch = []
+    for _, u, r, c in classes:
+        scratch += [
+            pltpu.VMEM((chips, u, r, c), jnp.bfloat16),
+            pltpu.VMEM((chips, u, r, c), jnp.bfloat16),
+            pltpu.VMEM((chips - 1, u, r, c), jnp.bfloat16),
+            pltpu.VMEM((chips - 1, u, r, c), jnp.bfloat16),
+            pltpu.SemaphoreType.DMA((chips, u)),
+            pltpu.SemaphoreType.DMA((chips, u)),
+            pltpu.SemaphoreType.DMA((chips - 1, u)),
+            pltpu.SemaphoreType.DMA((chips - 1, u)),
+        ]
+    return pl.pallas_call(
+        functools.partial(scatter_sum_kernel, n, len(arrays), classes),
+        out_shape=[
+            jax.ShapeDtypeStruct((u, r, c), t) for (_, u, r, c), t in zip(classes, out_types)
+        ],
+        in_specs=[VM] * len(arrays),
+        out_specs=[VM] * len(classes),
+        scratch_shapes=scratch,
+        compiler_params=pltpu.CompilerParams(collective_id=collective_id, has_side_effects=True),
+    )(*arrays)
+
+
+def attention_kernel(heads, block, q_ref, k_ref, v_ref, o_ref):
+    total = q_ref.shape[0]
+    for begin in range(0, total, block):
+        end = begin + block
+        keys = k_ref[:end, :]
+        values = v_ref[:end, :]
+        row = lax.broadcasted_iota(jnp.int32, (block, end), 0) + begin
+        col = lax.broadcasted_iota(jnp.int32, (block, end), 1)
+        for h in range(heads):
+            query = q_ref[begin:end, h * HEAD : (h + 1) * HEAD]
+            scores = lax.dot_general(
+                query, keys, (((1,), (1,)), ((), ())), preferred_element_type=jnp.float32
+            ) * (1.0 / math.sqrt(HEAD))
+            scores = jnp.where(col <= row, scores, -1e30)
+            top = jnp.max(scores, axis=-1, keepdims=True)
+            weights = jnp.exp(scores - top)
+            denominator = jnp.sum(weights, axis=-1, keepdims=True)
+            mix = jnp.dot(weights.astype(jnp.bfloat16), values, preferred_element_type=jnp.float32)
+            o_ref[begin:end, h * HEAD : (h + 1) * HEAD] = (mix / denominator).astype(o_ref.dtype)
+
+
+def body(
+    n,
+    hidden,
+    kept_idx,
+    kept_count,
+    router,
+    norm_gain,
+    qk_gain,
+    query_weight,
+    key_weight,
+    value_weight,
+    out_weight,
+):
+    device = lax.axis_index("blk")
+    tokens, width = hidden.shape
+    cap = kept_idx.shape[1]
+    part = width // n
+    slots = jnp.arange(cap, dtype=jnp.int32)
+    token_rows = hidden[kept_idx[0]]
+    gate_value = jax.nn.sigmoid(jnp.dot(token_rows, router, preferred_element_type=jnp.float32))
+    normed = rms_scale(token_rows.astype(jnp.float32), norm_gain).astype(jnp.bfloat16)
+    meta = jnp.concatenate(
+        [kept_idx, jnp.broadcast_to(kept_count[:, None], (7, cap))], axis=0
+    ).astype(jnp.int32)
+    rows_by_shard, metas = exchange(n, (normed, meta), (True, False), 1)
+    counts = metas[:, 1, 0]
+    lists = metas[:, 0, :]
+    starts = jnp.cumsum(counts) - counts
+    valid = slots[None, :] < counts[:, None]
+    keep = n * KEEP_OF(tokens)
+    ranks = jnp.where(valid, starts[:, None] + slots[None, :], keep).reshape(-1)
+    places = (jnp.arange(n, dtype=jnp.int32)[:, None] * tokens + lists).reshape(-1)
+    sel = ranks[None, :] == jnp.arange(keep, dtype=jnp.int32)[:, None]
+    positions = jnp.sum(jnp.where(sel, places[None, :], 0), axis=1)
+    rows = jnp.dot(
+        sel.astype(jnp.bfloat16),
+        rows_by_shard.reshape(n * cap, part),
+        preferred_element_type=jnp.float32,
+    ).astype(jnp.bfloat16)
+    own = keep // n
+    q_cols = Q_HEADS * HEAD // n
+    kv_cols = 2 * KV_HEADS * HEAD
+    q_units = 4
+    q_rows = keep // q_units
+    kv_rows = own // 2
+    kv_weight = jnp.concatenate([key_weight, value_weight], axis=1)
+
+    def query_chunk(ins, dest, u):
+        cols = pl.ds(pl.multiple_of(dest * q_cols, q_cols), q_cols)
+        return jnp.dot(
+            ins[0][u * q_rows : (u + 1) * q_rows, :],
+            ins[1][:, cols],
+            preferred_element_type=jnp.float32,
+        )
+
+    def kv_chunk(ins, dest, u):
+        at = pl.ds(pl.multiple_of(dest * own + u * kv_rows, kv_rows), kv_rows)
+        return jnp.dot(ins[0][at, :], ins[2][...], preferred_element_type=jnp.float32)
+
+    query_lin, kv_lin = scatter_sum(
+        n,
+        (rows, query_weight, kv_weight),
+        ((query_chunk, q_units, q_rows, q_cols), (kv_chunk, 2, kv_rows, kv_cols)),
+        (jnp.float32, jnp.float32),
+        2,
+    )
+    heads = Q_HEADS // n
+    query_lin = query_lin.reshape(keep, heads, HEAD)
+    kv_lin = kv_lin.reshape(own, 2 * KV_HEADS, HEAD)
+    half_size = HEAD // 2
+    rotation_rates = rope_base ** (-(jnp.arange(half_size, dtype=jnp.float32) * 2.0 / HEAD))
+    angles = (positions.astype(jnp.float32)[:, None] * rotation_rates[None, :])[:, None, :]
+    query_heads = rotate(rms_scale(query_lin, qk_gain[0]), angles).astype(jnp.bfloat16)
+    own_angles = lax.dynamic_slice_in_dim(angles, device * own, own, 0)
+    key_heads = rotate(rms_scale(kv_lin[:, :KV_HEADS], qk_gain[1]), own_angles).astype(jnp.bfloat16)
+    value_heads = kv_lin[:, KV_HEADS:].astype(jnp.bfloat16)
+    own_kv = jnp.concatenate(
+        [key_heads.reshape(own, KV_HEADS * HEAD), value_heads.reshape(own, KV_HEADS * HEAD)], axis=1
+    )
+    (all_kv,) = exchange(n, (own_kv,), (False,), 3)
+    all_kv = all_kv.reshape(keep, 2 * KV_HEADS, HEAD)
+    group = device * heads // (Q_HEADS // KV_HEADS)
+    keys = lax.dynamic_index_in_dim(all_kv, group, 1, keepdims=False)
+    values = lax.dynamic_index_in_dim(all_kv, KV_HEADS + group, 1, keepdims=False)
+    attended = pl.pallas_call(
+        functools.partial(attention_kernel, heads, math.gcd(keep, 256)),
+        out_shape=jax.ShapeDtypeStruct((keep, q_cols), jnp.bfloat16),
+        in_specs=[VM] * 3,
+        out_specs=VM,
+    )(query_heads.reshape(keep, q_cols), keys, values)
+    padded = lax.dot_general(
+        sel.astype(jnp.bfloat16), attended, (((0,), (0,)), ((), ())), preferred_element_type=jnp.float32
+    ).astype(jnp.bfloat16)
+    out_units = 4
+    out_rows = cap // out_units
+
+    def out_chunk(ins, dest, u):
+        at = pl.ds(pl.multiple_of(dest * cap + u * out_rows, out_rows), out_rows)
+        return jnp.dot(ins[0][at, :], ins[1][...], preferred_element_type=jnp.float32)
+
+    (update,) = scatter_sum(
+        n,
+        (padded, out_weight),
+        ((out_chunk, out_units, out_rows, width),),
+        (jnp.bfloat16,),
+        4,
+    )
+    update = update.reshape(cap, width).astype(jnp.float32)
+    final = (token_rows.astype(jnp.float32) + gate_value[:, None] * update).astype(jnp.bfloat16)
+    put = (kept_idx == jnp.arange(tokens, dtype=jnp.int32)[:, None]) & (slots[None, :] < kept_count[0])
+    placed = jnp.dot(put.astype(jnp.bfloat16), final, preferred_element_type=jnp.float32)
+    return jnp.where(jnp.any(put, axis=1)[:, None], placed.astype(jnp.bfloat16), hidden)
+
+
+def KEEP_OF(tokens):
+    return tokens * KEEP_DEV // TOK_DEV
 
 
 def attend(query_heads, query_ranks, key_block, value_block, key_ranks, state):
@@ -73,7 +391,7 @@
     return lax.fori_loop(0, length // 512, inner, state)
 
 
-def body(
+def wide_body(
     hidden,
     kept_idx,
     kept_count,
@@ -193,6 +511,9 @@
         P("blk", None),
         P("blk", None),
     )
+    n = mesh.shape["blk"]
+    by_heads = n % 4 == 0 and (Q_HEADS * HEAD // n) % 128 == 0
+    step = functools.partial(body, n) if by_heads else wide_body
     return jax.shard_map(
-        body, mesh=mesh, in_specs=placed, out_specs=P(("groups", "blk"), None), check_vma=False
-    )
+        step, mesh=mesh, in_specs=placed, out_specs=P(("groups", "blk"), None), check_vma=False
+    )

time: 216 us -> 162 us (0.75)
  Pallas kernels: 0 us -> 127 us
  blocking collectives: 123 us -> 0 us
  between operations: 17 us -> 0.88 us
  waiting for transfers between devices: 13.8 us -> 0 us
  matrix products: 22.3 us -> 10.8 us
  starting transfers between devices: 7.41 us -> 0 us
  other arithmetic: 14.6 us -> 7.48 us
    pallas_call x0 -> x5, Pallas kernels: none -> 127 us  [the longest x2 89.8 us: scatter_sum(): pl.pallas_call(functools.partial(scatter_sum_kernel, n, len(arrays), clas...]
    all_gather x5 -> x0, blocking collectives: 109 us -> none  [the longest x1 25.9 us: body(): lax.all_gather(kept_idx, 'blk', axis=0, tiled=True)]
    unnamed x1 -> x0, blocking collectives: 13.8 us -> none
    all_to_all x2 -> x0, waiting for transfers between devices: 13.1 us -> none  [the longest x1 13.1 us: body(): lax.all_to_all(back_rows, 'blk', split_axis=1, concat_axis=1, tiled=True)]
    dot_general x8 -> x3, matrix products: 22.1 us -> 10.6 us  [the longest x1 4.25 us: body(): lax.dot_general(sel.astype(jnp.bfloat16), attended, (((0,), (0,)), ((), (...]
    all_to_all x2 -> x0, starting transfers between devices: 7.36 us -> none  [the longest x1 3.79 us: body(): lax.all_to_all(back_rows, 'blk', split_axis=1, concat_axis=1, tiled=True)]
    reduce_sum x3 -> x1, other arithmetic: 7.04 us -> 0.91 us  [body(): positions = jnp.sum(jnp.where(sel, places[None, :], 0), axis=1)]
    scatter x1 -> x0, local copies, waits for them, and re-layouts: 4.62 us -> none  [body(): return hidden.at[target].set(final, mode='drop')]
  transfers between devices with their start and end apart: 4 -> 0, of which waited for: 1 -> 0; matrix products, arithmetic and copies ran while one was open for 18% -> 0% of each run, Pallas kernels for 0% -> 0%
where the time goes in v1:
time: 162 us; the launch traced here: 161 us
  Pallas kernels  127 us (78%)
  local copies, waits for them, and re-layouts  15.1 us (9%)
  matrix products  10.8 us (7%)
  other arithmetic  7.48 us (5%)
    pallas_call x2, Pallas kernels, scatter_sum(): pl.pallas_call(functools.partial(scatter_sum_kernel, n, len(arrays), clas...  89.8 us
    pallas_call x2, Pallas kernels, exchange(): pl.pallas_call(functools.partial(exchange_kernel, n, split), out_shape=ou...  31.8 us
    pallas_call x1, Pallas kernels, body(): pl.pallas_call(functools.partial(attention_kernel, heads, math.gcd(keep,...  5.16 us
    dot_general x1, matrix products, body(): lax.dot_general(sel.astype(jnp.bfloat16), attended, (((0,), (0,)), ((), (...  4.25 us
    gather x1, local copies, waits for them, and re-layouts, body(): token_rows = hidden[kept_idx[0]]  3.31 us

profile of v1, /device:TPU:0, one launch (start us, length us, event | category | flops | bytes accessed | tf_op | source)
XLA Modules:
  0.0 161.1 jit_solution(2368951565367912773)
XLA Ops:
  0.7 0.8 fusion.19
  1.5 0.7 fusion.22
  2.1 0.8 slice_bitcast_fusion
  2.9 1.2 concatenate.17.refs_1_
  4.2 0.7 reshape.243
  4.8 1.4 pad_maximum_fusion.1.refs_2_
  6.2 3.3 %gather_fusion = bf16[128,2048]{1,0:T(8,128)(2,1)S(1)} fusion(bf16[512,2048]{1,0:T(8,128)(2,1)} %param.10, s32[1024]{0:T(1024)S(1)} %pad_clamp_fusion), kind=kCustom, calls=%fused_computation | custom fusion | bytes 1049088 | tf_op jit(solution)/shard_map/gather | solution.py:257
  9.6 0.2 fusion.10
  9.8 0.2 fusion.11
  10.0 0.0 copy-done.2
  10.0 1.0 fusion.13.refs_0_
  11.0 18.5 %shard_map.100 = (bf16[16,128,128]{2,1,0:T(8,128)(2,1)}, s32[16,8,128]{2,1,0:T(8,128)}) custom-call(bf16[128,2048]{1,0:T(8,128)(2,1)} %fusion.13.refs_0_, s32[8,128]{1,0:T(8,128)} %concatenate.17.refs_1_), custom_call_target="tpu_custom_call" | custom-call | tf_op jit(solution)/shard_map/pallas_call | solution.py:100
  29.5 0.8 slice.34
  30.4 1.2 slice_reduce_fusion
  31.6 0.1 reduce.1
  31.8 0.1 bitcast_add_fusion
  31.8 0.1 select_bitcast_fusion
  31.9 3.2 %fusion.6.refs_0_ = bf16[1024,128]{1,0:T(8,128)(2,1)} fusion(bf16[2048,128]{1,0:T(8,128)(2,1)} %bitcast.48, s32[2048]{0:T(1024)S(1)} %select_bitcast_fusion), kind=kOutput, calls=%fused_computation.13 | convolution fusion | flops 539099136 | bytes 794624 | tf_op jit(solution)/shard_map/dot_general | solution.py:273
  35.1 0.9 select_reduce_fusion
  36.0 38.7 %shard_map.101 = (f32[4,256,128]{2,1,0:T(8,128)}, f32[2,32,256]{2,1,0:T(8,128)}) custom-call(bf16[1024,128]{1,0:T(8,128)(2,1)} %fusion.6.refs_0_, bf16[128,2048]{1,0:T(8,128)(2,1)} %refs_1_.2, bf16[128,256]{1,0:T(8,128)(2,1)} %pad_maximum_fusion.1.refs_2_), custom_call_target="tpu_custom_call" | custom-call | tf_op jit(solution)/shard_map/pallas_call | solution.py:206
  74.7 0.0 copy-start.1
  74.7 1.3 copy.40
  76.0 0.3 reshape.230
  76.3 0.1 multiply_reduce_fusion
  76.4 0.1 multiply_multiply_fusion
  76.5 0.0 copy-done.1
  76.5 0.1 reshape.231
  76.6 0.1 reshape.232
  76.7 0.1 multiply_reduce_fusion.1
  76.9 0.1 multiply_multiply_fusion.1
  77.0 0.7 broadcast_multiply_fusion
  77.7 0.1 subtract_convert_fusion
  77.8 0.1 dynamic-slice_cosine_fusion
  78.0 0.8 copy.48.q_ref
  78.8 0.1 copy.43
  78.9 0.1 copy.44
  79.0 0.2 subtract_convert_fusion.1
  79.2 0.1 pad_maximum_fusion.2
  79.3 0.1 convert_element_type.51
  79.4 0.6 pad_maximum_fusion.3.refs_0_
  80.0 13.3 %shard_map.102 = bf16[16,64,256]{2,1,0:T(8,128)(2,1)} custom-call(bf16[64,256]{1,0:T(8,128)(2,1)} %pad_maximum_fusion.3.refs_0_), custom_call_target="tpu_custom_call" | custom-call | tf_op jit(solution)/shard_map/pallas_call | solution.py:100
  93.4 2.0 %reshape.245 = bf16[1024,4,64]{2,1,0:T(4,128)(2,1)S(1)} reshape(bf16[16,64,256]{2,1,0:T(8,128)(2,1)} %shard_map.102) | data formatting | bytes 1048576 | tf_op jit(solution)/shard_map/reshape | solution.py:319
  95.4 1.1 constant_dynamic-slice_fusion
  96.5 0.9 copy_bitcast_fusion
  97.4 5.2 %shard_map.103 = bf16[1024,128]{1,0:T(8,128)(2,1)} custom-call(bf16[1024,128]{1,0:T(8,128)(2,1)} %copy.48.q_ref, bf16[1024,64]{1,0:T(8,128)(2,1)} %get-tuple-element.29.k_ref, bf16[1024,64]{1,0:T(8,128)(2,1)} %get-tuple-element.28.v_ref), custom_call_target="tpu_custom_call" | custom-call | tf_op jit(solution)/shard_map/pallas_call | solution.py:323
  102.5 4.3 %fusion.5.refs_0_ = bf16[2048,128]{1,0:T(8,128)(2,1)} fusion(bf16[1024,128]{1,0:T(8,128)(2,1)} %shard_map.103, s32[2048]{0:T(1024)S(1)} %select_bitcast_fusion), kind=kOutput, calls=%fused_computation.9 | convolution fusion | flops 539230208 | bytes 794624 | tf_op jit(solution)/shard_map/dot_general | solution.py:329
  106.8 51.2 %shard_map.104 = bf16[4,32,2048]{2,1,0:T(8,128)(2,1)} custom-call(bf16[2048,128]{1,0:T(8,128)(2,1)} %fusion.5.refs_0_, bf16[128,2048]{1,0:T(8,128)(2,1)} %refs_1_.3), custom_call_target="tpu_custom_call" | custom-call | tf_op jit(solution)/shard_map/pallas_call | solution.py:206
  158.0 3.2 %fusion.4 = bf16[512,2048]{1,0:T(8,128)(2,1)} fusion(bf16[512,2048]{1,0:T(8,128)(2,1)S(1)} %copy-done, pred[512]{0:T(512)(128)(4,1)S(1)} %fusion.19, bf16[128,2048]{1,0:T(8,128)(2,1)S(1)} %gather_fusion, bf16[128,2048]{1,0:T(8,128)(2,1)} %bitcast.42, f32[128]{0:T(128)S(1)} %fusion.10, s32[128]{0:T(128)S(1)} %bitcast.47, pred[128]{0:T(512)(128)(4,1)S(1)} %iota_compare_fusion.9), kind=kOutput, calls=%fused_computation.8 | convolution fusion | flops 271974400 | bytes 5244544 | tf_op jit(solution)/shard_map/dot_general | solution.py:349
  (17 shorter events, 0.2 us)
Async XLA Ops:
  6.2 3.8 %copy-start.2 = (f32[2048]{0:T(1024)S(1)}, f32[2048]{0:T(1024)}, u32[]{:S(2)}) copy-start(f32[2048]{0:T(1024)} %param.14) | copy-start | bytes 24580
  74.7 1.8 %copy-start.1 = (f32[2,32,256]{2,1,0:T(8,128)S(1)}, f32[2,32,256]{2,1,0:T(8,128)}, u32[]{:S(2)}) copy-start(f32[2,32,256]{2,1,0:T(8,128)} %get-tuple-element.12) | copy-start | bytes 196612
  102.5 55.4 %copy-start = (bf16[512,2048]{1,0:T(8,128)(2,1)S(1)}, bf16[512,2048]{1,0:T(8,128)(2,1)}, u32[]{:S(2)}) copy-start(bf16[512,2048]{1,0:T(8,128)(2,1)} %param.10) | copy-start | bytes 6291460
  102.5 55.4 %copy-start.3 = (s32[1,128]{1,0:T(1,128)S(1)}, s32[1,128]{1,0:T(1,128)}, u32[]{:S(2)}) copy-start(s32[1,128]{1,0:T(1,128)} %param.11) | copy-start | bytes 1540

commit v2 on v0

--- a/solution.py
+++ b/solution.py
@@ -1,8 +1,11 @@
+import functools
 import math
 
 import jax
 import jax.numpy as jnp
 from jax import lax
+from jax.experimental import pallas as pl
+from jax.experimental.pallas import tpu as pltpu
 from jax.sharding import PartitionSpec as P
 
 Q_HEADS = 32
@@ -11,6 +14,8 @@
 TOK_DEV = 512
 KEEP_DEV = 64
 CAP = 128
+MESH = pl.DeviceIdType.MESH
+VM = pl.BlockSpec(memory_space=pltpu.VMEM)
 
 
 norm_eps = 1e-06
@@ -34,6 +39,423 @@
         ],
         axis=-1,
     )
+
+
+def greet(peers):
+    barrier = pltpu.get_barrier_semaphore()
+    for peer in peers:
+        pl.semaphore_signal(barrier, inc=1, device_id={"blk": peer}, device_id_type=MESH)
+    pl.semaphore_wait(barrier, len(peers))
+
+
+def spread_kernel(n, hidden_ref, idx_ref, count_ref, gain_ref, out_ref, metas_ref, rows_ref, x_buf, meta_buf, send_sem, recv_sem):
+    me = lax.axis_index("blk")
+    part = out_ref.shape[-1]
+    barrier = pltpu.get_barrier_semaphore()
+    for o in range(1, n):
+        pl.semaphore_signal(
+            barrier, inc=1, device_id={"blk": lax.rem(me + o, n)}, device_id_type=MESH
+        )
+    tokens, cap = hidden_ref.shape[0], idx_ref.shape[1]
+    pick = lax.broadcasted_iota(jnp.int32, (tokens, cap), 0) == idx_ref[...]
+    rows = lax.dot_general(
+        pick.astype(jnp.float32).astype(jnp.bfloat16),
+        hidden_ref[...],
+        (((0,), (0,)), ((), ())),
+        preferred_element_type=jnp.float32,
+    )
+    rows_ref[...] = rows.astype(jnp.bfloat16)
+    x_buf[...] = rms_scale(rows, gain_ref[...]).astype(jnp.bfloat16)
+    line = lax.broadcasted_iota(jnp.int32, meta_buf.shape, 0)
+    meta_buf[...] = jnp.where(line == 0, idx_ref[...], count_ref[...])
+
+    def copies(o, dest, place):
+        cols = pl.ds(pl.multiple_of(dest * part, part), part)
+        pairs = ((x_buf.at[:, cols], out_ref), (meta_buf, metas_ref))
+        return [
+            pltpu.make_async_remote_copy(
+                src_ref=src,
+                dst_ref=dst.at[place],
+                send_sem=send_sem.at[i, o],
+                recv_sem=recv_sem.at[i, o],
+                device_id={"blk": dest},
+                device_id_type=MESH,
+            )
+            for i, (src, dst) in enumerate(pairs)
+        ]
+
+    pl.semaphore_wait(barrier, n - 1)
+    started = []
+    for o in range(1, n):
+        for copy in copies(o, lax.rem(me + o, n), me):
+            copy.start()
+            started.append(copy)
+    out_ref[me] = x_buf[:, pl.ds(pl.multiple_of(me * part, part), part)]
+    metas_ref[me] = meta_buf[...]
+    for o in range(1, n):
+        source = lax.rem(me + n - o, n)
+        for copy in copies(o, source, source):
+            copy.wait_recv()
+    for copy in started:
+        copy.wait_send()
+
+
+def spread(n, hidden, kept_idx, kept_count, norm_gain):
+    width, cap = hidden.shape[1], kept_idx.shape[1]
+    return pl.pallas_call(
+        functools.partial(spread_kernel, n),
+        out_shape=[
+            jax.ShapeDtypeStruct((n, cap, width // n), jnp.bfloat16),
+            jax.ShapeDtypeStruct((n, 8, cap), jnp.int32),
+            jax.ShapeDtypeStruct((cap, width), jnp.bfloat16),
+        ],
+        in_specs=[VM] * 4,
+        out_specs=[VM] * 3,
+        scratch_shapes=[
+            pltpu.VMEM((cap, width), jnp.bfloat16),
+            pltpu.VMEM((8, cap), jnp.int32),
+            pltpu.SemaphoreType.DMA((2, n)),
+            pltpu.SemaphoreType.DMA((2, n)),
+        ],
+        compiler_params=pltpu.CompilerParams(collective_id=1, has_side_effects=True),
+    )(hidden, kept_idx, kept_count.reshape(1, 1), norm_gain.reshape(1, width))
+
+
+class Ring:
+    def __init__(self, n):
+        self.chips = n // 2
+        self.arm = self.chips // 2
+        self.me = lax.axis_index("blk")
+        self.chip, self.core = self.me // 2, self.me % 2
+        side, row = self.chip % 2, self.chip // 2
+        self.place = row * (1 - side) + (self.chips - 1 - row) * side
+        self.partner = self.chip * 2 + 1 - self.core
+        self.ahead = self.device(self.place + 1, self.core)
+        self.behind = self.device(self.place - 1, self.core)
+
+    def device(self, position, on_core):
+        q = lax.rem(position + 2 * self.chips, self.chips)
+        far = q // self.arm
+        chip_id = 2 * (q * (1 - far) + (self.chips - 1 - q) * far) + far
+        return chip_id * 2 + on_core
+
+    def target(self, step, u):
+        return self.place - 1 - step if u % 2 == 0 else self.place + 1 + step
+
+
+class RingSum:
+    def __init__(self, ring, chunk, units, bufs, finish):
+        self.ring, self.chunk, self.units, self.bufs, self.finish = ring, chunk, units, bufs, finish
+
+    @staticmethod
+    def scratch(chips, u, r, c):
+        return [
+            pltpu.VMEM((chips, u, r, c), jnp.bfloat16),
+            pltpu.VMEM((chips, u, r, c), jnp.bfloat16),
+            pltpu.VMEM((chips - 1, u, r, c), jnp.bfloat16),
+            pltpu.VMEM((chips - 1, u, r, c), jnp.bfloat16),
+            pltpu.SemaphoreType.DMA((chips, u)),
+            pltpu.SemaphoreType.DMA((chips, u)),
+            pltpu.SemaphoreType.DMA((chips - 1, u)),
+            pltpu.SemaphoreType.DMA((chips - 1, u)),
+        ]
+
+    def copy(self, pair, step, u):
+        pair_out, pair_in, ring_out, ring_in, ps, pr, rs, rr = self.bufs
+        src, dst, ss, sr = (pair_out, pair_in, ps, pr) if pair else (ring_out, ring_in, rs, rr)
+        to = self.ring.partner if pair else (self.ring.ahead if u % 2 == 0 else self.ring.behind)
+        return pltpu.make_async_remote_copy(
+            src_ref=src.at[step, u],
+            dst_ref=dst.at[step, u],
+            send_sem=ss.at[step, u],
+            recv_sem=sr.at[step, u],
+            device_id={"blk": to},
+            device_id_type=MESH,
+        )
+
+    def pair_send(self, step):
+        ring = self.ring
+        for u in range(self.units):
+            dest = ring.device(ring.target(step, u), 1 - ring.core)
+            self.bufs[0][step, u] = self.chunk(dest, u).astype(jnp.bfloat16)
+            self.copy(True, step, u).start()
+
+    def advance(self, step):
+        ring = self.ring
+        for u in range(self.units):
+            total = self.chunk(ring.device(ring.target(step, u), ring.core), u)
+            self.copy(True, step, u).wait_recv()
+            total = total + self.bufs[1][step, u].astype(jnp.float32)
+            if step > 0:
+                self.copy(False, step - 1, u).wait_recv()
+                total = total + self.bufs[3][step - 1, u].astype(jnp.float32)
+            if step + 1 < ring.chips:
+                self.bufs[2][step, u] = total.astype(jnp.bfloat16)
+                self.copy(False, step, u).start()
+            else:
+                self.finish(u, total)
+
+    def drain(self):
+        for step in range(self.ring.chips):
+            for u in range(self.units):
+                self.copy(True, step, u).wait_send()
+                if step + 1 < self.ring.chips:
+                    self.copy(False, step, u).wait_send()
+
+
+def turn(values, cosine, sine, lane):
+    swapped = jnp.where(lane % HEAD < HEAD // 2, pltpu.roll(values, 2 * HEAD - HEAD // 2, 1), pltpu.roll(values, HEAD // 2, 1))
+    return values * cosine + swapped * sine
+
+
+def attend_kernel(n, tokens, q_units, x_ref, metas_ref, wq_ref, wk_ref, wv_ref, gain_ref, rate_ref, padded_ref,
+                  x_buf, pos_buf, kvp_buf, kv_lin, own_kv, all_kv, q_buf, att_buf, cos_buf, sin_buf,
+                  kv_send, kv_recv, *bufs):
+    ring = Ring(n)
+    me, chips = ring.me, ring.chips
+    barrier = pltpu.get_barrier_semaphore()
+    for o in range(1, n):
+        pl.semaphore_signal(
+            barrier, inc=1, device_id={"blk": lax.rem(me + o, n)}, device_id_type=MESH
+        )
+    cap = x_ref.shape[1]
+    keep = x_buf.shape[0]
+    own = keep // n
+    lanes = 2 * HEAD
+    q_rows, kv_rows = keep // q_units, own // 2
+
+    starts, counts = [], []
+    start = jnp.zeros((1, cap), jnp.int32)
+    for s in range(n):
+        count = metas_ref[s, 1:2, :]
+        starts.append(start)
+        counts.append(count)
+        start = start + count
+    slot = lax.broadcasted_iota(jnp.int32, (1, cap), 1)
+    block = 256
+    for b in range(keep // block):
+        rank = lax.broadcasted_iota(jnp.int32, (block, cap), 0) + b * block
+        total = jnp.zeros((block, x_buf.shape[1]), jnp.float32)
+        places = jnp.zeros((block, cap), jnp.float32)
+        for s in range(n):
+            rank_row = jnp.where(slot < counts[s], starts[s] + slot, keep)
+            hit = rank == rank_row
+            place_row = (metas_ref[s, 0:1, :] + s * tokens).astype(jnp.float32)
+            places = places + jnp.where(hit, place_row, 0.0)
+            total = total + jnp.dot(
+                hit.astype(jnp.float32).astype(jnp.bfloat16), x_ref[s], preferred_element_type=jnp.float32
+            )
+        x_buf[b * block : (b + 1) * block, :] = total.astype(jnp.bfloat16)
+        pos_buf[b * block : (b + 1) * block, :] = jnp.broadcast_to(
+            jnp.sum(places, axis=1, keepdims=True), (block, lanes)
+        )
+    for g in range(KV_HEADS):
+        weight = jnp.concatenate(
+            [wk_ref[:, g * HEAD : (g + 1) * HEAD], wv_ref[:, g * HEAD : (g + 1) * HEAD]], axis=1
+        )
+        kvp_buf[:, g * lanes : (g + 1) * lanes] = jnp.dot(
+            x_buf[...], weight, preferred_element_type=jnp.float32
+        )
+
+    def query_chunk(dest, u):
+        cols = pl.ds(pl.multiple_of(dest * lanes, lanes), lanes)
+        return jnp.dot(
+            x_buf[u * q_rows : (u + 1) * q_rows, :], wq_ref[:, cols], preferred_element_type=jnp.float32
+        )
+
+    def kv_chunk(dest, u):
+        return kvp_buf[pl.ds(pl.multiple_of(dest * own + u * kv_rows, kv_rows), kv_rows), :]
+
+    def kv_finish(u, total):
+        kv_lin[u * kv_rows : (u + 1) * kv_rows, :] = total
+
+    lane = lax.broadcasted_iota(jnp.int32, (1, lanes), 1)
+    sign = jnp.where(lane % HEAD < HEAD // 2, -1.0, 1.0)
+
+    def query_finish(u, total):
+        gain = jnp.concatenate([gain_ref[0:1, :], gain_ref[0:1, :]], axis=1)
+        squares = total * total
+        first = jnp.sum(jnp.where(lane < HEAD, squares, 0.0), axis=1, keepdims=True)
+        second = jnp.sum(jnp.where(lane < HEAD, 0.0, squares), axis=1, keepdims=True)
+        mean = jnp.where(lane < HEAD, first, second) * (1.0 / HEAD)
+        values = total * lax.rsqrt(mean + norm_eps) * gain
+        at = slice(u * q_rows, (u + 1) * q_rows)
+        q_buf[at, :] = turn(values, cos_buf[at, :], sin_buf[at, :], lane).astype(jnp.bfloat16)
+
+    kv_ring = RingSum(ring, kv_chunk, 2, bufs[:8], kv_finish)
+    q_ring = RingSum(ring, query_chunk, q_units, bufs[8:], query_finish)
+
+    def kv_copy(o, dest, place):
+        return pltpu.make_async_remote_copy(
+            src_ref=own_kv.at[dest * KV_HEADS // n],
+            dst_ref=all_kv.at[place],
+            send_sem=kv_send.at[o],
+            recv_sem=kv_recv.at[o],
+            device_id={"blk": dest},
+            device_id_type=MESH,
+        )
+
+    def share():
+        angle = pos_buf[pl.ds(pl.multiple_of(me * own, own), own), :] * rate_ref[...]
+        cosine, sine = jnp.cos(angle), jnp.sin(angle) * sign
+        gain = jnp.concatenate([gain_ref[1:2, :], gain_ref[1:2, :]], axis=1)
+        for g in range(KV_HEADS):
+            both = kv_lin[:, g * lanes : (g + 1) * lanes]
+            mean = jnp.sum(jnp.where(lane < HEAD, both * both, 0.0), axis=1, keepdims=True) * (1.0 / HEAD)
+            key = turn(both * lax.rsqrt(mean + norm_eps) * gain, cosine, sine, lane)
+            own_kv[g] = jnp.where(lane < HEAD, key, both).astype(jnp.bfloat16)
+        for o in range(1, n):
+            kv_copy(o, lax.rem(me + o, n), me).start()
+        all_kv[me] = own_kv[me * KV_HEADS // n]
+
+    pl.semaphore_wait(barrier, n - 1)
+    kv_ring.pair_send(0)
+    kv_ring.pair_send(1)
+    q_ring.pair_send(0)
+    table = keep // chips
+    for step in range(chips):
+        for k in (2 * step, 2 * step + 1):
+            if k < chips:
+                kv_ring.advance(k)
+                if k + 2 < chips:
+                    kv_ring.pair_send(k + 2)
+                if k + 1 == chips:
+                    share()
+        if step + 1 < chips:
+            q_ring.pair_send(step + 1)
+        rows = slice(step * table, (step + 1) * table)
+        angle = pos_buf[rows, :] * rate_ref[...]
+        cos_buf[rows, :] = jnp.cos(angle)
+        sin_buf[rows, :] = jnp.sin(angle) * sign
+        q_ring.advance(step)
+    for o in range(1, n):
+        source = lax.rem(me + n - o, n)
+        kv_copy(o, source, source).wait_recv()
+
+    for begin in range(0, keep, block):
+        end = begin + block
+        pairs = all_kv[: end // own].reshape(end, lanes)
+        row = lax.broadcasted_iota(jnp.int32, (block, end), 0) + begin
+        col = lax.broadcasted_iota(jnp.int32, (block, end), 1)
+        both = q_buf[begin:end, :].astype(jnp.float32)
+        mixes = []
+        for h in range(2):
+            query = jnp.where(lane < HEAD, both if h == 0 else pltpu.roll(both, HEAD, 1), 0.0)
+            scores = lax.dot_general(
+                query.astype(jnp.bfloat16), pairs, (((1,), (1,)), ((), ())), preferred_element_type=jnp.float32
+            ) * (1.0 / math.sqrt(HEAD))
+            scores = jnp.where(col <= row, scores, -1e30)
+            top = jnp.max(scores, axis=-1, keepdims=True)
+            weights = jnp.exp(scores - top)
+            denominator = jnp.sum(weights, axis=-1, keepdims=True)
+            mix = jnp.dot(weights.astype(jnp.bfloat16), pairs, preferred_element_type=jnp.float32)
+            mixes.append(mix / denominator)
+        att_buf[begin:end, :] = jnp.where(lane < HEAD, pltpu.roll(mixes[0], HEAD, 1), mixes[1]).astype(jnp.bfloat16)
+
+    offset = lax.broadcasted_iota(jnp.int32, (cap, keep), 1) - lax.broadcasted_iota(jnp.int32, (cap, keep), 0)
+    for s in range(n):
+        hit = offset == starts[s][:, 0:1]
+        padded_ref[s * cap : (s + 1) * cap, :] = jnp.dot(
+            hit.astype(jnp.float32).astype(jnp.bfloat16), att_buf[...], preferred_element_type=jnp.float32
+        ).astype(jnp.bfloat16)
+    kv_ring.drain()
+    q_ring.drain()
+    for o in range(1, n):
+        kv_copy(o, lax.rem(me + o, n), me).wait_send()
+
+
+def attend_shards(n, tokens, keep, by_shard, metas, query_weight, key_weight, value_weight, qk_gain):
+    cap, part = by_shard.shape[1:]
+    lanes, own, chips, q_units = 2 * HEAD, keep // n, n // 2, 4
+    half_size = HEAD // 2
+    rates = rope_base ** (-(jnp.arange(half_size, dtype=jnp.float32) * 2.0 / HEAD))
+    rates = jnp.tile(rates, lanes // half_size)[None, :]
+    return pl.pallas_call(
+        functools.partial(attend_kernel, n, tokens, q_units),
+        out_shape=jax.ShapeDtypeStruct((n * cap, lanes), jnp.bfloat16),
+        in_specs=[VM] * 7,
+        out_specs=VM,
+        scratch_shapes=[
+            pltpu.VMEM((keep, part), jnp.bfloat16),
+            pltpu.VMEM((keep, lanes), jnp.float32),
+            pltpu.VMEM((keep, KV_HEADS * lanes), jnp.float32),
+            pltpu.VMEM((own, KV_HEADS * lanes), jnp.float32),
+            pltpu.VMEM((KV_HEADS, own, lanes), jnp.bfloat16),
+            pltpu.VMEM((n, own, lanes), jnp.bfloat16),
+            pltpu.VMEM((keep, lanes), jnp.bfloat16),
+            pltpu.VMEM((keep, lanes), jnp.bfloat16),
+            pltpu.VMEM((keep, lanes), jnp.float32),
+            pltpu.VMEM((keep, lanes), jnp.float32),
+            pltpu.SemaphoreType.DMA((n,)),
+            pltpu.SemaphoreType.DMA((n,)),
+        ]
+        + RingSum.scratch(chips, 2, own // 2, KV_HEADS * lanes)
+        + RingSum.scratch(chips, q_units, keep // q_units, lanes),
+        compiler_params=pltpu.CompilerParams(collective_id=2, has_side_effects=True),
+    )(by_shard, metas, query_weight, key_weight, value_weight, qk_gain, rates)
+
+
+def deliver_kernel(n, units, padded_ref, weight_ref, out_ref, *bufs):
+    ring = Ring(n)
+    greet([ring.partner, ring.ahead, ring.behind])
+    cap = padded_ref.shape[0] // n
+    rows = cap // units
+
+    def chunk(dest, u):
+        at = pl.ds(pl.multiple_of(dest * cap + u * rows, rows), rows)
+        return jnp.dot(padded_ref[at, :], weight_ref[...], preferred_element_type=jnp.float32)
+
+    def finish(u, total):
+        out_ref[u * rows : (u + 1) * rows, :] = total.astype(out_ref.dtype)
+
+    summed = RingSum(ring, chunk, units, bufs, finish)
+    summed.pair_send(0)
+    for step in range(ring.chips):
+        if step + 1 < ring.chips:
+            summed.pair_send(step + 1)
+        summed.advance(step)
+    summed.drain()
+
+
+def deliver(n, padded, out_weight):
+    cap, width, units = padded.shape[0] // n, out_weight.shape[1], 4
+    return pl.pallas_call(
+        functools.partial(deliver_kernel, n, units),
+        out_shape=jax.ShapeDtypeStruct((cap, width), jnp.bfloat16),
+        in_specs=[VM] * 2,
+        out_specs=VM,
+        scratch_shapes=RingSum.scratch(n // 2, units, cap // units, width),
+        compiler_params=pltpu.CompilerParams(collective_id=4, has_side_effects=True),
+    )(padded, out_weight)
+
+
+def body(
+    n,
+    hidden,
+    kept_idx,
+    kept_count,
+    router,
+    norm_gain,
+    qk_gain,
+    query_weight,
+    key_weight,
+    value_weight,
+    out_weight,
+):
+    tokens = hidden.shape[0]
+    cap = kept_idx.shape[1]
+    keep = n * (tokens * KEEP_DEV // TOK_DEV)
+    by_shard, metas, token_rows = spread(n, hidden, kept_idx, kept_count, norm_gain)
+    padded = attend_shards(
+        n, tokens, keep, by_shard, metas, query_weight, key_weight, value_weight, qk_gain
+    )
+    gate_value = jax.nn.sigmoid(jnp.dot(token_rows, router, preferred_element_type=jnp.float32))
+    update = deliver(n, padded, out_weight).astype(jnp.float32)
+    final = (token_rows.astype(jnp.float32) + gate_value[:, None] * update).astype(jnp.bfloat16)
+    slots = jnp.arange(cap, dtype=jnp.int32)
+    put = (kept_idx == jnp.arange(tokens, dtype=jnp.int32)[:, None]) & (slots[None, :] < kept_count[0])
+    placed = jnp.dot(put.astype(jnp.bfloat16), final, preferred_element_type=jnp.float32)
+    return jnp.where(jnp.any(put, axis=1)[:, None], placed.astype(jnp.bfloat16), hidden)
 
 
 def attend(query_heads, query_ranks, key_block, value_block, key_ranks, state):
@@ -73,7 +495,7 @@
     return lax.fori_loop(0, length // 512, inner, state)
 
 
-def body(
+def wide_body(
     hidden,
     kept_idx,
     kept_count,
@@ -193,6 +615,9 @@
         P("blk", None),
         P("blk", None),
     )
+    n = mesh.shape["blk"]
+    by_heads = n % 4 == 0 and Q_HEADS == 2 * n
+    step = functools.partial(body, n) if by_heads else wide_body
     return jax.shard_map(
-        body, mesh=mesh, in_specs=placed, out_specs=P(("groups", "blk"), None), check_vma=False
-    )
+        step, mesh=mesh, in_specs=placed, out_specs=P(("groups", "blk"), None), check_vma=False
+    )

time: 216 us -> 131 us (0.61)
  Pallas kernels: 0 us -> 124 us
  blocking collectives: 123 us -> 0 us
  matrix products: 22.3 us -> 4.6 us
  between operations: 17 us -> 0.75 us
  local copies, waits for them, and re-layouts: 16.5 us -> 1.33 us
  waiting for transfers between devices: 13.8 us -> 0 us
  other arithmetic: 14.6 us -> 0.82 us
  starting transfers between devices: 7.41 us -> 0 us
    pallas_call x0 -> x3, Pallas kernels: none -> 124 us  [the longest x1 56.8 us: attend_shards(): pl.pallas_call(functools.partial(attend_kernel, n, tokens, q_units), out_...]
    all_gather x5 -> x0, blocking collectives: 109 us -> none  [the longest x1 25.9 us: body(): lax.all_gather(kept_idx, 'blk', axis=0, tiled=True)]
    dot_general x8 -> x1, matrix products: 22.1 us -> 3.16 us  [body(): jnp.dot(put.astype(jnp.bfloat16), final, preferred_element_type=jnp.float32)]
    unnamed x1 -> x0, blocking collectives: 13.8 us -> none
    all_to_all x2 -> x0, waiting for transfers between devices: 13.1 us -> none  [the longest x1 13.1 us: body(): lax.all_to_all(back_rows, 'blk', split_axis=1, concat_axis=1, tiled=True)]
    reduce_sum x6 -> x0, other arithmetic: 7.69 us -> none  [the longest x2 6.96 us: attend(): new_total = prev_total * factor + jnp.sum(weights, axis=-1)]
    all_to_all x2 -> x0, starting transfers between devices: 7.36 us -> none  [the longest x1 3.79 us: body(): lax.all_to_all(back_rows, 'blk', split_axis=1, concat_axis=1, tiled=True)]
    scatter x1 -> x0, local copies, waits for them, and re-layouts: 4.62 us -> none  [body(): return hidden.at[target].set(final, mode='drop')]
  transfers between devices with their start and end apart: 4 -> 0, of which waited for: 1 -> 0; matrix products, arithmetic and copies ran while one was open for 18% -> 0% of each run, Pallas kernels for 0% -> 0%
where the time goes in v2:
time: 131 us
  Pallas kernels  124 us (95%)
  matrix products  4.6 us (4%)
  local copies, waits for them, and re-layouts  1.33 us (1%)
    pallas_call x1, Pallas kernels, attend_shards(): pl.pallas_call(functools.partial(attend_kernel, n, tokens, q_units), out_...  56.8 us
    pallas_call x1, Pallas kernels, deliver(): pl.pallas_call(functools.partial(deliver_kernel, n, units), out_shape=jax...  47.7 us
    pallas_call x1, Pallas kernels, spread(): pl.pallas_call(functools.partial(spread_kernel, n), out_shape=[jax.ShapeD...  19.2 us
    dot_general x1, matrix products, body(): jnp.dot(put.astype(jnp.bfloat16), final, preferred_element_type=jnp.float32)  3.16 us

profile of v2, /device:TPU:0, one launch (start us, length us, event | category | flops | bytes accessed | tf_op | source)
XLA Modules:
  0.0 131.2 jit_solution(2045748624209078610)
XLA Ops:
  0.7 0.8 fusion.8
  1.5 0.6 broadcast_in_dim_tile.3.rate_ref
  2.1 0.7 reshape.21
  2.8 19.2 %shard_map.100 = (bf16[16,128,128]{2,1,0:T(8,128)(2,1)}, s32[16,8,128]{2,1,0:T(8,128)}, bf16[128,2048]{1,0:T(8,128)(2,1)}) custom-call(bf16[512,2048]{1,0:T(8,128)(2,1)} %hidden_ref.1, s32[1,128]{1,0:T(1,128)} %idx_ref.1, s32[1,1]{1,0:T(1,128)} %bitcast.17.count_ref, f32[1,2048]{1,0:T(1,128)} %bitcast.18), custom_call_target="tpu_custom_call" | custom-call | tf_op jit(solution)/shard_map/pallas_call | solution.py:105
  22.1 0.0 copy-start
  22.1 0.0 copy-start.1
  22.1 0.0 copy-start.2
  22.1 1.4 %fusion.4 = f32[128]{0:T(128)S(1)} fusion(bf16[128,2048]{1,0:T(8,128)(2,1)} %get-tuple-element.8, bf16[2048,1]{0,1:T(2,128)(2,1)S(1)} %reshape.21), kind=kOutput, calls=%fused_computation.6 | convolution fusion | flops 524672 | bytes 528896 | tf_op jit(solution)/shard_map/dot_general | solution.py:452
  23.5 56.8 %shard_map.101.padded_ref = bf16[2048,128]{1,0:T(8,128)(2,1)} custom-call(bf16[16,128,128]{2,1,0:T(8,128)(2,1)} %get-tuple-element.9.x_ref, s32[16,8,128]{2,1,0:T(8,128)} %get-tuple-element.10.metas_ref, bf16[128,2048]{1,0:T(8,128)(2,1)} %wq_ref.1, bf16[128,128]{1,0:T(8,128)(2,1)} %wk_ref.1, bf16[128,128]{1,0:T(8,128)(2,1)} %wv_ref.1, f32[2,64]{1,0:T(2,128)} %gain_ref.1, ...), custom_call_target="tpu_custom_call" | custom-call | tf_op jit(solution)/shard_map/pallas_call | solution.py:373
  80.3 47.7 %shard_map.102 = bf16[128,2048]{1,0:T(8,128)(2,1)} custom-call(bf16[2048,128]{1,0:T(8,128)(2,1)} %shard_map.101.padded_ref, bf16[128,2048]{1,0:T(8,128)(2,1)} %weight_ref.1), custom_call_target="tpu_custom_call" | custom-call | tf_op jit(solution)/shard_map/pallas_call | solution.py:422
  128.0 0.0 copy-done
  128.0 0.0 copy-done.1
  128.0 0.0 copy-done.2
  128.0 3.2 %fusion = bf16[512,2048]{1,0:T(8,128)(2,1)} fusion(bf16[512,2048]{1,0:T(8,128)(2,1)S(1)} %copy-done, pred[512]{0:T(512)(128)(4,1)S(1)} %fusion.8, bf16[128,2048]{1,0:T(8,128)(2,1)} %shard_map.102, bf16[128,2048]{1,0:T(8,128)(2,1)S(1)} %copy-done.1, f32[128]{0:T(128)S(1)} %fusion.4, s32[128]{0:T(128)S(1)} %bitcast.20, pred[128]{0:T(512)(128)(4,1)S(1)} %iota_compare_fusion.1), kind=kOutput, calls=%fused_computation.1 | convolution fusion | flops 271974400 | bytes 5244544 | tf_op jit(solution)/shard_map/dot_general | solution.py:457
  (3 shorter events, 0.0 us)
Async XLA Ops:
  22.1 105.9 %copy-start = (bf16[512,2048]{1,0:T(8,128)(2,1)S(1)}, bf16[512,2048]{1,0:T(8,128)(2,1)}, u32[]{:S(2)}) copy-start(bf16[512,2048]{1,0:T(8,128)(2,1)} %hidden_ref.1) | copy-start | bytes 6291460
  22.1 105.9 %copy-start.1 = (bf16[128,2048]{1,0:T(8,128)(2,1)S(1)}, bf16[128,2048]{1,0:T(8,128)(2,1)}, u32[]{:S(2)}) copy-start(bf16[128,2048]{1,0:T(8,128)(2,1)} %get-tuple-element.8) | copy-start | bytes 1572868
  22.1 105.9 %copy-start.2 = (s32[1,128]{1,0:T(1,128)S(1)}, s32[1,128]{1,0:T(1,128)}, u32[]{:S(2)}) copy-start(s32[1,128]{1,0:T(1,128)} %idx_ref.1) | copy-start | bytes 1540
